TPU v7x, 32 devices: a whole 2x2x4 slice. The times are simulated.
32 devices in a mesh: dp: 4 (over x, core), seq: 8 (over z, y).
Axes of the slice: x: 2, y: 2, z: 4, core: 2. Of those that a mesh axis runs over, the one named last changes fastest.
Arguments:
- spatial_input: bfloat16 [4, 8, 64, 256], P('dp', 'seq'), may hold values from -6 to 6
- temporal_input: bfloat16 [4, 64, 8, 256], P('dp', 'seq'), may hold values from -6 to 6
- out_cotangent: bfloat16 [4, 8, 64, 256], P('dp', 'seq'), may hold values from -6 to 6
- weights: bfloat16 [2, 256, 1024], replicated, may hold values from -3 to 3
- gains: float32 [2, 256], replicated, may hold values from 0.1 to 1.9
Outputs:
- input_grad: bfloat16 [4, 8, 64, 256], P('dp', 'seq')
- weight_grads: float32 [2, 262144], P(None, ('dp', 'seq'))
- gain_grads: float32 [2, 256], replicated
All inputs are finite; a program needn't handle non-finite values.
Results may differ from a plain program's by a relative error of at most 0.023.
Values may be sent and summed in bfloat16 or wider, within the bound.
A program may use at most 64 MiB of HBM per device.

v0:
```python
from functools import partial
import math
import jax
import jax.numpy as jnp
from jax import lax
from jax.sharding import PartitionSpec as P

HEADS = 4


def one_head(head_parts, score_scale):
    query_rows, key_rows, value_rows = head_parts
    scores = (
        jnp.einsum("gqe,gke->gqk", query_rows, key_rows, preferred_element_type=jnp.float32)
        * score_scale
    )
    probs = jax.nn.softmax(scores, axis=-1).astype(jnp.bfloat16)
    return jnp.einsum("gqk,gke->gqe", probs, value_rows, preferred_element_type=jnp.float32).astype(
        jnp.bfloat16
    )


def attend_block(block_input, gain_vector, weight, head_count):
    groups, length, model_width = block_input.shape
    head_size = model_width // head_count
    mean_sq = jnp.mean(block_input * block_input, axis=-1, keepdims=True)
    normed = (block_input * lax.rsqrt(mean_sq + 1e-06) * gain_vector).astype(jnp.bfloat16)
    w_cast = weight.astype(jnp.bfloat16)
    packed = jnp.dot(
        normed.reshape(groups * length, model_width),
        w_cast[:, : 3 * model_width],
        preferred_element_type=jnp.float32,
    ).astype(jnp.bfloat16)
    packed = jnp.transpose(
        packed.reshape(groups, length, 3, head_count, head_size), (2, 3, 0, 1, 4)
    )
    head_fn = jax.checkpoint(partial(one_head, score_scale=1.0 / math.sqrt(head_size)))
    mixed_heads = lax.map(head_fn, (packed[0], packed[1], packed[2]))
    mixed_heads = jnp.transpose(mixed_heads, (1, 2, 0, 3)).reshape(groups * length, model_width)
    result = jnp.dot(mixed_heads, w_cast[:, 3 * model_width :], preferred_element_type=jnp.float32)
    return result.reshape(groups, length, model_width)


def per_device(spatial_input, temporal_input, out_cotangent, weights, gains):
    w_float = weights.astype(jnp.float32)
    block_fn = partial(attend_block, head_count=HEADS)
    sample_count = spatial_input.shape[0] * lax.axis_size("dp")
    frame_count = spatial_input.shape[1] * lax.axis_size("seq")
    patch_count = spatial_input.shape[2]
    grad_factor = 1.0 / math.sqrt(sample_count * frame_count * patch_count)
    patch_major = jnp.swapaxes(out_cotangent[0], 0, 1)
    temporal_cot = lax.all_to_all(
        patch_major, "seq", split_axis=0, concat_axis=1, tiled=True
    ).astype(jnp.float32)
    unused_t, pullback_t = jax.vjp(
        block_fn, temporal_input[0].astype(jnp.float32), gains[1], w_float[1]
    )
    grad_ut, grad_gt, grad_wt = pullback_t(temporal_cot)
    temporal_term = (grad_wt * grad_factor).reshape(1, -1)
    mid_grad = (temporal_cot + grad_ut).astype(jnp.bfloat16)
    frame_back = lax.all_to_all(mid_grad, "seq", split_axis=1, concat_axis=0, tiled=True)
    spatial_cot = jnp.swapaxes(frame_back, 0, 1).astype(jnp.float32)
    unused_s, pullback_s = jax.vjp(
        block_fn, spatial_input[0].astype(jnp.float32), gains[0], w_float[0]
    )
    grad_us, grad_gs, grad_ws = pullback_s(spatial_cot)
    input_grad = (spatial_cot + grad_us).astype(jnp.bfloat16)[None]
    spatial_term = (grad_ws * grad_factor).reshape(1, -1)
    both_terms = jnp.concatenate([spatial_term, temporal_term], axis=0)
    grid_terms = both_terms.reshape(2, lax.axis_size("dp"), lax.axis_size("seq"), -1)
    over_frames = lax.psum_scatter(
        grid_terms.astype(jnp.bfloat16), "seq", scatter_dimension=2, tiled=True
    ).astype(jnp.float32)
    over_frames = over_frames.reshape(2, lax.axis_size("dp"), -1)
    weight_grads = (
        lax.psum_scatter(over_frames.astype(jnp.bfloat16), "dp", scatter_dimension=1, tiled=True)
        .astype(jnp.float32)
        .reshape(2, -1)
    )
    gain_grads = lax.psum(jnp.stack([grad_gs, grad_gt]) * grad_factor, ("dp", "seq"))
    return (input_grad, weight_grads, gain_grads)


def solution(mesh):
    return jax.shard_map(
        per_device,
        mesh=mesh,
        in_specs=(
            P("dp", "seq", None, None),
            P("dp", "seq", None, None),
            P("dp", "seq", None, None),
            P(),
            P(),
        ),
        out_specs=(P("dp", "seq", None, None), P(None, ("dp", "seq")), P()),
        check_vma=False,
    )
```

profile of v0, /device:TPU:0, one launch (start us, length us, event | category | flops | bytes accessed | tf_op | source)
XLA Modules:
  0.0 179.6 jit_solution(7019148246470243943)
XLA Ops:
  7.2 0.5 broadcast.288
  7.7 1.4 reduce.34
  9.1 0.6 reshape.395
  9.7 7.4 %all-to-all-start = ((bf16[8,2,1024]{2,1,0:T(2,128)(2,1)}), bf16[8,2,1024]{2,1,0:T(2,128)(2,1)S(1)}, u32[]{:S(2)}, u32[]{:S(2)}) async-start(bf16[8,2,1024]{2,1,0:T(2,128)(2,1)} %reshape.395), calls=%async_computation | async-start | bytes 65536 | tf_op jit(solution)/shard_map/all_to_all | solution.py:52
  17.3 0.7 copy-done.1
  18.1 0.6 copy-done.2
  18.9 1.3 slice_bitcast_fusion.1
  20.6 2.0 %while.59 = (s32[]{:T(128)}, bf16[4,8,8,64]{3,2,1,0:T(8,128)(2,1)S(1)}, bf16[4,8,8,64]{3,2,1,0:T(8,128)(2,1)S(1)}, bf16[4,8,8,64]{3,2,1,0:T(8,128)(2,1)S(1)}, bf16[4,8,8,64]{3,2,1,0:T(8,128)(2,1)S(1)}, /*index=5*/s32[]{:T(128)}) while((s32[]{:T(128)}, bf16[4,8,8,64]{3,2,1,0:T(8,128)(2,1)S(1)}, bf16[4,8,8,64]{3,2,1,0:T(8,128)(2,1)S(1)}, ...), condition=%wide.region_21.22_spmd, body=%wide.region_18.0_spmd.sunk | while | flops 204368 | bytes 105805 | solution.py:38
  20.8 0.3 fusion.234
  21.3 0.3 fusion.234
  21.8 0.3 fusion.234
  22.3 0.3 fusion.234
  23.1 1.6 while.58
  25.6 4.9 %while.56 = (s32[]{:T(128)}, bf16[4,8,8,64]{3,2,1,0:T(8,128)(2,1)S(1)}, bf16[4,8,8,64]{3,2,1,0:T(8,128)(2,1)S(1)}, bf16[4,8,8,64]{3,2,1,0:T(8,128)(2,1)S(1)}, bf...) while((s32[]{:T(128)}, ...), condition=%wide.region_5.6_spmd, body=%wide.region_1.5_spmd.sunk | while | flops 549215 | bytes 388997 | solution.py:38
  25.9 0.3 fusion.215
  26.2 0.3 fusion.214
  26.5 0.3 fusion.213
  27.2 0.3 fusion.215
  27.4 0.3 fusion.214
  27.7 0.3 fusion.213
  28.4 0.3 fusion.215
  28.6 0.3 fusion.214
  28.9 0.3 fusion.213
  29.6 0.3 fusion.215
  29.9 0.3 fusion.214
  30.1 0.3 fusion.213
  30.9 0.3 fusion.84
  31.3 0.7 fusion.99
  32.0 6.0 %all-to-all-start.1 = ((bf16[8,8,256]{2,0,1:T(8,128)(2,1)}), bf16[8,8,256]{2,0,1:T(8,128)(2,1)S(1)}, u32[]{:S(2)}, u32[]{:S(2)}) async-start(bf16[8,8,256]{2,0,1:T(8,128)(2,1)} %fusion.99), calls=%async_computation.1 | async-start | bytes 65536 | tf_op jit(solution)/shard_map/all_to_all | solution.py:61
  38.2 0.3 convolution_convert_fusion.10
  38.6 0.2 concatenate.10
  38.9 0.4 copy.103
  39.3 5.4 %all-to-all-done.1 = bf16[8,8,256]{2,0,1:T(8,128)(2,1)S(1)} async-done(((bf16[8,8,256]{2,0,1:T(8,128)(2,1)}), bf16[8,8,256]{2,0,1:T(8,128)(2,1)S(1)}, u32[]{:S(2)}, u32[]{:S(2)}) %all-to-all-start.1) | async-done | bytes 32800 | tf_op jit(solution)/shard_map/all_to_all | solution.py:61
  45.0 4.7 %while.57 = (s32[]{:T(128)}, bf16[4,1,64,64]{2,3,0,1:T(8,128)(2,1)S(1)}, bf16[4,1,64,64]{2,3,0,1:T(8,128)(2,1)S(1)}, bf16[4,1,64,64]{2,3,1,0:T(8,128)(2,1)S(1)},...) while((s32[]{:T(128)}, ...), condition=%wide.region_12.13_spmd, body=%wide.region_8.12_spmd.sunk | while | flops 2727939 | bytes 431237 | solution.py:38
  49.8 0.4 convolution_convert_fusion.11
  50.4 0.2 concatenate.9
  50.7 0.4 copy.102
  51.1 1.7 pad_maximum_fusion
  52.9 0.6 copy-done.4
  53.6 0.6 dynamic-slice.2
  54.2 0.6 dynamic-slice
  54.8 0.4 fusion.97
  55.2 0.7 fusion.117
  55.9 72.8 %all-reduce.15.cloned.1.call-done = bf16[2,4,8,8192]{3,1,0,2:T(4,128)(2,1)} async-done(((bf16[2,4,8,8192]{3,1,0,2:T(4,128)(2,1)}), bf16[2,4,8,8192]{3,1,0,2:T(4,128)(2,1)}) %all-reduce.15.cloned.1.call-update) | async-done | bytes 1048592
  128.7 1.6 dynamic-slice_bitcast_fusion.8
  130.3 0.8 copy.104
  131.1 39.6 %psum.7 = f32[2,256]{1,0:T(2,128)} all-reduce(f32[2,256]{1,0:T(2,128)S(1)} %maximum_multiply_fusion), channel_id=1, replica_groups=mesh['dp'=4,'seq'=8] {'dp','seq'}, use_global_device_ids=true, to_apply=%region_26.27 | all-reduce | flops 512 | bytes 4096 | tf_op jit(solution)/shard_map/psum | solution.py:80
  170.7 2.0 %bitcast_convert_fusion = f32[2,8192]{1,0:T(2,128)} fusion(bf16[2,4,8192]{2,0,1:T(2,128)(2,1)} %all-reduce.17.cloned.1.call-done, u32[]{:T(128)} %bitcast.79), kind=kLoop, calls=%fused_computation.171 | loop fusion | flops 16384 | bytes 98308 | tf_op jit(solution)/shard_map/reshape | solution.py:78
  (158 shorter events, 11.6 us)
Async XLA Ops:
  9.7 7.4 %copy-start = (bf16[1,8,8,256]{3,2,1,0:T(8,128)(2,1)S(1)}, bf16[1,8,8,256]{3,2,1,0:T(8,128)(2,1)}, u32[]{:S(2)}) copy-start(bf16[1,8,8,256]{3,2,1,0:T(8,128)(2,1)} %param.14) | copy-start | bytes 98308
  9.7 15.4 %all-to-all-start = ((bf16[8,2,1024]{2,1,0:T(2,128)(2,1)}), bf16[8,2,1024]{2,1,0:T(2,128)(2,1)S(1)}, u32[]{:S(2)}, u32[]{:S(2)}) async-start(bf16[8,2,1024]{2,1,0:T(2,128)(2,1)} %reshape.395), calls=%async_computation | async-start | bytes 65536 | tf_op jit(solution)/shard_map/all_to_all | solution.py:52
  17.3 0.8 copy-start.1
  18.0 0.7 copy-start.2
  32.0 12.7 %all-to-all-start.1 = ((bf16[8,8,256]{2,0,1:T(8,128)(2,1)}), bf16[8,8,256]{2,0,1:T(8,128)(2,1)S(1)}, u32[]{:S(2)}, u32[]{:S(2)}) async-start(bf16[8,8,256]{2,0,1:T(8,128)(2,1)} %fusion.99), calls=%async_computation.1 | async-start | bytes 65536 | tf_op jit(solution)/shard_map/all_to_all | solution.py:61
  38.0 90.8 %all-reduce.15.cloned.1.call-start = ((), (), s32[]{:S(2)}) async-start(), calls=%async_computation.2 | async-start | bytes 2097152
  52.9 117.9 %all-reduce.17.cloned.1.call-start = ((), (), s32[]{:S(2)}) async-start(), calls=%async_computation.3 | async-start | bytes 262144
  52.9 0.7 copy-start.4
  53.6 0.7 copy-start.3
Sparse Core Ops, SparseCore 0:
  53.0 75.6 all-reduce.14
  131.2 31.3 all-reduce.16
where the time goes:
time: 180 us
  waiting for transfers between devices  78.2 us (43%)
  blocking collectives  39.6 us (22%)
  between operations  14.4 us (8%)
  matrix products  13.7 us (8%)
  starting transfers between devices  13.5 us (8%)
  local copies, waits for them, and re-layouts  12 us (7%)
  other arithmetic  7.74 us (4%)
    unnamed x4, waiting for transfers between devices  72.8 us
    psum x1, blocking collectives, per_device(): lax.psum(jnp.stack([grad_gs, grad_gt]) * grad_factor, ('dp', 'seq'))  39.6 us
    all_to_all x1, starting transfers between devices, per_device(): lax.all_to_all(patch_major, 'seq', split_axis=0, concat_axis=1, tiled=True)  7.44 us
    all_to_all x1, starting transfers between devices, per_device(): lax.all_to_all(mid_grad, 'seq', split_axis=1, concat_axis=0, tiled=True)  5.99 us
    all_to_all x1, waiting for transfers between devices, per_device(): lax.all_to_all(mid_grad, 'seq', split_axis=1, concat_axis=0, tiled=True)  5.36 us
    dot_general x24, matrix products, one_head(): jnp.einsum('gqk,gke->gqe', probs, value_rows, preferred_element_type=jnp....  5.11 us
    dot_general x24, matrix products, one_head(): jnp.einsum('gqe,gke->gqk', query_rows, key_rows, preferred_element_type=j...  4.94 us
    unnamed x15, local copies, waits for them, and re-layouts  3.85 us
  transfers between devices with their start and end apart: 4, of which 2 were waited for; matrix products, arithmetic and copies ran while one was open for 6% of the time, Pallas kernels for 0%

commit v1 on v0

--- a/solution.py
+++ b/solution.py
@@ -77,7 +77,7 @@
         .astype(jnp.float32)
         .reshape(2, -1)
     )
-    gain_grads = lax.psum(jnp.stack([grad_gs, grad_gt]) * grad_factor, ("dp", "seq"))
+    gain_grads = lax.psum(lax.psum(jnp.stack([grad_gs, grad_gt]) * grad_factor, "dp"), "seq")
     return (input_grad, weight_grads, gain_grads)
 
 

time: 180 us -> 172 us (0.956)
  blocking collectives: 39.6 us -> 26.5 us
  waiting for transfers between devices: 78.2 us -> 83.2 us
    psum x1 -> x2, blocking collectives: 39.6 us -> 26.5 us  [the longest x1 20 us: per_device(): lax.psum(lax.psum(jnp.stack([grad_gs, grad_gt]) * grad_factor, 'dp'), 'seq')]
    unnamed x4, waiting for transfers between devices: 72.8 us -> 77.8 us
  transfers between devices with their start and end apart: 4 -> 4, of which waited for: 2 -> 3; matrix products, arithmetic and copies ran while one was open for 6% -> 6% of each run, Pallas kernels for 0% -> 0%
where the time goes in v1:
time: 172 us
  waiting for transfers between devices  83.2 us (48%)
  blocking collectives  26.5 us (15%)
  between operations  14.4 us (8%)
  matrix products  13.7 us (8%)
  starting transfers between devices  13.5 us (8%)
  local copies, waits for them, and re-layouts  12 us (7%)
  other arithmetic  7.74 us (4%)
    unnamed x4, waiting for transfers between devices  77.8 us
    psum x1, blocking collectives, per_device(): lax.psum(lax.psum(jnp.stack([grad_gs, grad_gt]) * grad_factor, 'dp'), 'seq')  20 us
    all_to_all x1, starting transfers between devices, per_device(): lax.all_to_all(patch_major, 'seq', split_axis=0, concat_axis=1, tiled=True)  7.44 us
    psum x1, blocking collectives, per_device(): lax.psum(jnp.stack([grad_gs, grad_gt]) * grad_factor, 'dp')  6.51 us
    all_to_all x1, starting transfers between devices, per_device(): lax.all_to_all(mid_grad, 'seq', split_axis=1, concat_axis=0, tiled=True)  5.99 us
    all_to_all x1, waiting for transfers between devices, per_device(): lax.all_to_all(mid_grad, 'seq', split_axis=1, concat_axis=0, tiled=True)  5.36 us
    dot_general x24, matrix products, one_head(): jnp.einsum('gqk,gke->gqe', probs, value_rows, preferred_element_type=jnp....  5.11 us
    dot_general x24, matrix products, one_head(): jnp.einsum('gqe,gke->gqk', query_rows, key_rows, preferred_element_type=j...  4.94 us
  transfers between devices with their start and end apart: 4, of which 3 were waited for; matrix products, arithmetic and copies ran while one was open for 6% of the time, Pallas kernels for 0%

profile of v1, /device:TPU:0, one launch (start us, length us, event | category | flops | bytes accessed | tf_op | source)
XLA Modules:
  0.0 171.5 jit_solution(4637782065453445164)
XLA Ops:
  7.2 0.5 broadcast.288
  7.7 1.4 reduce.34
  9.1 0.6 reshape.395
  9.7 7.4 %all-to-all-start = ((bf16[8,2,1024]{2,1,0:T(2,128)(2,1)}), bf16[8,2,1024]{2,1,0:T(2,128)(2,1)S(1)}, u32[]{:S(2)}, u32[]{:S(2)}) async-start(bf16[8,2,1024]{2,1,0:T(2,128)(2,1)} %reshape.395), calls=%async_computation | async-start | bytes 65536 | tf_op jit(solution)/shard_map/all_to_all | solution.py:52
  17.3 0.7 copy-done.1
  18.1 0.6 copy-done.2
  18.9 1.3 slice_bitcast_fusion.1
  20.6 2.0 %while.59 = (s32[]{:T(128)}, bf16[4,8,8,64]{3,2,1,0:T(8,128)(2,1)S(1)}, bf16[4,8,8,64]{3,2,1,0:T(8,128)(2,1)S(1)}, bf16[4,8,8,64]{3,2,1,0:T(8,128)(2,1)S(1)}, bf16[4,8,8,64]{3,2,1,0:T(8,128)(2,1)S(1)}, /*index=5*/s32[]{:T(128)}) while((s32[]{:T(128)}, bf16[4,8,8,64]{3,2,1,0:T(8,128)(2,1)S(1)}, bf16[4,8,8,64]{3,2,1,0:T(8,128)(2,1)S(1)}, ...), condition=%wide.region_21.22_spmd, body=%wide.region_18.0_spmd.sunk | while | flops 204368 | bytes 105805 | solution.py:38
  20.8 0.3 fusion.234
  21.3 0.3 fusion.234
  21.8 0.3 fusion.234
  22.3 0.3 fusion.234
  23.1 1.6 while.58
  25.6 4.9 %while.56 = (s32[]{:T(128)}, bf16[4,8,8,64]{3,2,1,0:T(8,128)(2,1)S(1)}, bf16[4,8,8,64]{3,2,1,0:T(8,128)(2,1)S(1)}, bf16[4,8,8,64]{3,2,1,0:T(8,128)(2,1)S(1)}, bf...) while((s32[]{:T(128)}, ...), condition=%wide.region_5.6_spmd, body=%wide.region_1.5_spmd.sunk | while | flops 549215 | bytes 388997 | solution.py:38
  25.9 0.3 fusion.215
  26.2 0.3 fusion.214
  26.5 0.3 fusion.213
  27.2 0.3 fusion.215
  27.4 0.3 fusion.214
  27.7 0.3 fusion.213
  28.4 0.3 fusion.215
  28.6 0.3 fusion.214
  28.9 0.3 fusion.213
  29.6 0.3 fusion.215
  29.9 0.3 fusion.214
  30.1 0.3 fusion.213
  30.9 0.3 fusion.84
  31.3 0.7 fusion.99
  32.0 6.0 %all-to-all-start.1 = ((bf16[8,8,256]{2,0,1:T(8,128)(2,1)}), bf16[8,8,256]{2,0,1:T(8,128)(2,1)S(1)}, u32[]{:S(2)}, u32[]{:S(2)}) async-start(bf16[8,8,256]{2,0,1:T(8,128)(2,1)} %fusion.99), calls=%async_computation.1 | async-start | bytes 65536 | tf_op jit(solution)/shard_map/all_to_all | solution.py:61
  38.2 0.3 convolution_convert_fusion.10
  38.9 0.4 copy.103
  39.3 5.4 %all-to-all-done.1 = bf16[8,8,256]{2,0,1:T(8,128)(2,1)S(1)} async-done(((bf16[8,8,256]{2,0,1:T(8,128)(2,1)}), bf16[8,8,256]{2,0,1:T(8,128)(2,1)S(1)}, u32[]{:S(2)}, u32[]{:S(2)}) %all-to-all-start.1) | async-done | bytes 32800 | tf_op jit(solution)/shard_map/all_to_all | solution.py:61
  45.0 4.7 %while.57 = (s32[]{:T(128)}, bf16[4,1,64,64]{2,3,0,1:T(8,128)(2,1)S(1)}, bf16[4,1,64,64]{2,3,0,1:T(8,128)(2,1)S(1)}, bf16[4,1,64,64]{2,3,1,0:T(8,128)(2,1)S(1)},...) while((s32[]{:T(128)}, ...), condition=%wide.region_12.13_spmd, body=%wide.region_8.12_spmd.sunk | while | flops 2727939 | bytes 431237 | solution.py:38
  49.8 0.4 convolution_convert_fusion.11
  50.7 0.4 copy.102
  51.1 1.7 %pad_maximum_fusion = bf16[2,4,8,8192]{3,1,0,2:T(4,128)(2,1)} fusion(bf16[1,4,8,8192]{3,1,0,2:T(4,128)(2,1)S(1)} %copy.103, bf16[1,4,8,8192]{3,1,0,2:T(4,128)(2,1)S(1)} %copy.102), kind=kLoop, calls=%fused_computation.110 | loop fusion | flops 524288 | bytes 2097152 | tf_op jit(solution)/shard_map/concatenate | solution.py:69
  52.9 0.6 copy-done.4
  53.6 0.6 dynamic-slice.2
  54.2 0.6 dynamic-slice
  54.8 0.4 fusion.97
  55.2 0.7 fusion.117
  55.9 72.8 %all-reduce.15.cloned.1.call-done = bf16[2,4,8,8192]{3,1,0,2:T(4,128)(2,1)} async-done(((bf16[2,4,8,8192]{3,1,0,2:T(4,128)(2,1)}), bf16[2,4,8,8192]{3,1,0,2:T(4,128)(2,1)}) %all-reduce.15.cloned.1.call-update) | async-done | bytes 1048592
  128.7 1.6 dynamic-slice_bitcast_fusion.8
  130.3 0.8 copy.104
  131.1 6.5 %psum.14 = f32[2,256]{1,0:T(2,128)S(1)} all-reduce(f32[2,256]{1,0:T(2,128)S(1)} %maximum_multiply_fusion), channel_id=1, replica_groups=mesh['dp'=4,'seq'=8] {'dp'}, use_global_device_ids=true, to_apply=%region_26.27 | all-reduce | flops 512 | bytes 4096 | tf_op jit(solution)/shard_map/psum | solution.py:80
  137.6 20.0 %psum.15 = f32[2,256]{1,0:T(2,128)} all-reduce(f32[2,256]{1,0:T(2,128)S(1)} %psum.14), channel_id=1, replica_groups=mesh['dp'=4,'seq'=8] {'seq'}, use_global_device_ids=true, to_apply=%region_27.28 | all-reduce | flops 512 | bytes 4096 | tf_op jit(solution)/shard_map/psum | solution.py:80
  157.6 5.0 %all-reduce.17.cloned.1.call-done = bf16[2,4,8192]{2,0,1:T(2,128)(2,1)} async-done(((bf16[2,4,8192]{2,0,1:T(2,128)(2,1)}), bf16[2,4,8192]{2,0,1:T(2,128)(2,1)}) %all-reduce.17.cloned.1.call-update) | async-done | bytes 131088
  162.7 2.0 %bitcast_convert_fusion = f32[2,8192]{1,0:T(2,128)} fusion(bf16[2,4,8192]{2,0,1:T(2,128)(2,1)} %all-reduce.17.cloned.1.call-done, u32[]{:T(128)} %bitcast.79), kind=kLoop, calls=%fused_computation.171 | loop fusion | flops 16384 | bytes 98308 | tf_op jit(solution)/shard_map/reshape | solution.py:78
  (159 shorter events, 12.1 us)
Async XLA Ops:
  9.7 7.4 %copy-start = (bf16[1,8,8,256]{3,2,1,0:T(8,128)(2,1)S(1)}, bf16[1,8,8,256]{3,2,1,0:T(8,128)(2,1)}, u32[]{:S(2)}) copy-start(bf16[1,8,8,256]{3,2,1,0:T(8,128)(2,1)} %param.14) | copy-start | bytes 98308
  9.7 15.4 %all-to-all-start = ((bf16[8,2,1024]{2,1,0:T(2,128)(2,1)}), bf16[8,2,1024]{2,1,0:T(2,128)(2,1)S(1)}, u32[]{:S(2)}, u32[]{:S(2)}) async-start(bf16[8,2,1024]{2,1,0:T(2,128)(2,1)} %reshape.395), calls=%async_computation | async-start | bytes 65536 | tf_op jit(solution)/shard_map/all_to_all | solution.py:52
  17.3 0.8 copy-start.1
  18.0 0.7 copy-start.2
  32.0 12.7 %all-to-all-start.1 = ((bf16[8,8,256]{2,0,1:T(8,128)(2,1)}), bf16[8,8,256]{2,0,1:T(8,128)(2,1)S(1)}, u32[]{:S(2)}, u32[]{:S(2)}) async-start(bf16[8,8,256]{2,0,1:T(8,128)(2,1)} %fusion.99), calls=%async_computation.1 | async-start | bytes 65536 | tf_op jit(solution)/shard_map/all_to_all | solution.py:61
  38.0 90.8 %all-reduce.15.cloned.1.call-start = ((), (), s32[]{:S(2)}) async-start(), calls=%async_computation.2 | async-start | bytes 2097152
  52.9 109.8 %all-reduce.17.cloned.1.call-start = ((), (), s32[]{:S(2)}) async-start(), calls=%async_computation.3 | async-start | bytes 262144
  52.9 0.7 copy-start.4
  53.6 0.7 copy-start.3
Sparse Core Ops, SparseCore 0:
  53.0 75.6 all-reduce.14
  131.2 31.3 all-reduce.16
